TPU v7x, 32 devices: a whole 2x2x4 slice. The times are simulated.
32 devices in a mesh: seq: 8 (over z, x), exp: 4 (over y, core).
Axes of the slice: x: 2, y: 2, z: 4, core: 2. Of those that a mesh axis runs over, the one named last changes fastest.
Arguments:
- residual: bfloat16 [4096, 8192], P('seq', 'exp'), may hold values from -16 to 16
- queries: bfloat16 [4096, 4096], P('seq', 'exp'), may hold values from -6 to 6
- keys: bfloat16 [4096, 4096], P('seq', 'exp'), may hold values from -10 to 10
- values: bfloat16 [4096, 4096], P('seq', 'exp'), may hold values from -6 to 6
- documents: int32 [4096], replicated, may hold values from 0 to 1, as said below
- out_proj: bfloat16 [4096, 8192], P(None, 'exp'), may hold values from -0.09375 to 0.09375
- modality: int32 [4096], P('seq'), may hold values from 0 to 1, as said below
- norm_gain: float32 [2, 8192], P(None, 'exp'), may hold values from 0.25 to 1.75
- picks: int32 [4, 64], replicated, may hold values from 0 to 4095, as said below
- router: bfloat16 [8192, 4], P(None, 'exp'), may hold values from -0.0625 to 0.0625
- w_gate: bfloat16 [4, 8192, 4096], P('exp', None, 'seq'), may hold values from -0.0625 to 0.0625
- w_up: bfloat16 [4, 8192, 4096], P('exp', None, 'seq'), may hold values from -0.0625 to 0.0625
- w_down: bfloat16 [4, 4096, 8192], P('exp', 'seq'), may hold values from -0.09375 to 0.09375
Outputs:
- layer_out: bfloat16 [4096, 8192], P('seq', 'exp')
Inputs may be any that keep to these rules, and one draw needn't show every extreme that they name: `modality`: 0 marks a text token, 1 an image token. `documents`: 0 for the first document, 1 for the second; the second begins between position 1024 and 3072. `picks`: row e lists 64 different positions in ascending order; all carry modality 0 for e < 2 and modality 1 otherwise. Within each aligned block of 512 positions (the tokens of one index of seq) a row lists at most 16 positions, and every row lists exactly 16 in some block.
All inputs are finite; a program needn't handle non-finite values.
Results may differ from a plain program's by a relative error of at most 0.0035.
Values may be sent and summed in bfloat16 or wider, within the bound.
A program may use at most 128 MiB of HBM per device.

v0:
```python
import math
import jax
import jax.numpy as jnp
from jax import lax
from jax.sharding import PartitionSpec as P

D = 8192
HD = 128
block_rows = 512


def shards(
    residual,
    queries,
    keys,
    values,
    documents,
    out_proj,
    modality,
    norm_gain,
    picks,
    router,
    w_gate,
    w_up,
    w_down,
):
    tokens = queries.shape[0]
    heads_here = queries.shape[1] // HD
    seq_pos = lax.axis_index("seq")
    start_row = seq_pos * tokens
    query_pos = start_row + jnp.arange(tokens, dtype=jnp.int32)
    query_doc = lax.dynamic_slice_in_dim(documents, start_row, tokens, 0)
    query_heads = queries.reshape(tokens, heads_here, HD)
    score_scale = 1.0 / math.sqrt(HD)

    def attend(state, key_rows, value_rows, key_start):
        row_count = key_rows.shape[0]
        key_pos = key_start + jnp.arange(row_count, dtype=jnp.int32)
        key_doc = lax.dynamic_slice_in_dim(documents, key_start, row_count, 0)
        scores = (
            jnp.einsum(
                "qhd,khd->qhk",
                query_heads,
                key_rows.reshape(row_count, heads_here, HD),
                preferred_element_type=jnp.float32,
            )
            * score_scale
        )
        allowed = (key_pos[None, :] <= query_pos[:, None]) & (
            key_doc[None, :] == query_doc[:, None]
        )
        scores = jnp.where(allowed[:, None, :], scores, -jnp.inf)
        running_max, running_sum, running_out = state
        new_max = jnp.maximum(running_max, jnp.max(scores, axis=2))
        factor = jnp.exp(running_max - new_max)
        weights = jnp.exp(scores - new_max[:, :, None])
        running_sum = running_sum * factor + jnp.sum(weights, axis=2)
        running_out = running_out * factor[:, :, None] + jnp.einsum(
            "qhk,khd->qhd",
            weights.astype(jnp.bfloat16),
            value_rows.reshape(row_count, heads_here, HD),
            preferred_element_type=jnp.float32,
        )
        return (new_max, running_sum, running_out)

    def visit_block(state, key_rows, value_rows, key_start):
        row_count = key_rows.shape[0]
        last_doc = lax.dynamic_index_in_dim(documents, key_start + row_count - 1, 0, keepdims=False)
        beyond = (key_start > query_pos[tokens - 1]) | (last_doc < query_doc[0])
        return lax.cond(
            beyond,
            lambda inner_state: inner_state,
            lambda inner_state: attend(inner_state, key_rows, value_rows, key_start),
            state,
        )

    initial = (
        jnp.full((tokens, heads_here), -1e30, jnp.float32),
        jnp.zeros((tokens, heads_here), jnp.float32),
        jnp.zeros((tokens, heads_here, HD), jnp.float32),
    )
    state = initial
    key_piece = lax.all_gather(keys, "seq", axis=0, tiled=True)
    value_piece = lax.all_gather(values, "seq", axis=0, tiled=True)
    row_count = key_piece.shape[0]
    blocks = row_count // block_rows
    key_stack = key_piece.reshape(blocks, block_rows, key_piece.shape[1])
    value_stack = value_piece.reshape(blocks, block_rows, value_piece.shape[1])

    def scan_step(inner_state, block_item):
        block_index, key_rows, value_rows = block_item
        return (visit_block(inner_state, key_rows, value_rows, block_index * block_rows), None)

    state, unused = lax.scan(
        scan_step, state, (jnp.arange(blocks, dtype=jnp.int32), key_stack, value_stack)
    )
    running_max, running_sum, running_out = state
    attended = (
        (running_out / running_sum[:, :, None])
        .reshape(tokens, heads_here * HD)
        .astype(jnp.bfloat16)
    )
    mixed = jnp.dot(
        lax.all_gather(attended, "exp", axis=1, tiled=True),
        out_proj,
        preferred_element_type=jnp.float32,
    )
    hidden_state = (residual.astype(jnp.float32) + mixed).astype(jnp.bfloat16)
    hidden_wide = hidden_state.astype(jnp.float32)
    square_total = lax.psum(jnp.sum(hidden_wide * hidden_wide, axis=1), "exp")
    inverse = lax.rsqrt(square_total / D + 1e-05)
    gain_rows = jnp.where(modality[:, None] == 0, norm_gain[0][None, :], norm_gain[1][None, :])
    normed = (hidden_wide * inverse[:, None] * gain_rows).astype(jnp.bfloat16)
    capacity = tokens // 32
    inside = (picks >= start_row) & (picks < start_row + tokens)
    slot_index = jnp.cumsum(inside.astype(jnp.int32), axis=1) - 1
    matched = inside[:, None, :] & (
        slot_index[:, None, :] == jnp.arange(capacity, dtype=jnp.int32)[None, :, None]
    )
    local_index = jnp.sum(jnp.where(matched, picks[:, None, :] - start_row, 0), axis=2)
    filled = jnp.any(matched, axis=2)
    rows_out = jnp.take(normed, local_index.T, axis=0)
    rows_out = jnp.where(filled.T[:, :, None], rows_out, jnp.zeros_like(rows_out))
    arrived = lax.all_to_all(rows_out, "exp", split_axis=1, concat_axis=1, tiled=True)
    expert_rows = arrived.reshape(capacity, D)
    logits = jnp.dot(expert_rows, router, preferred_element_type=jnp.float32)[:, 0]
    piece = lax.all_gather(expert_rows, "seq", axis=0, tiled=True)
    gate_part = jnp.dot(piece, w_gate[0], preferred_element_type=jnp.float32)
    up_part = jnp.dot(piece, w_up[0], preferred_element_type=jnp.float32)
    inner_act = (jax.nn.silu(gate_part) * up_part).astype(jnp.bfloat16)
    summed = lax.psum_scatter(
        jnp.dot(inner_act, w_down[0], preferred_element_type=jnp.float32).astype(jnp.bfloat16),
        "seq",
        scatter_dimension=0,
        tiled=True,
    ).astype(jnp.float32)
    weighted = (jax.nn.sigmoid(logits)[:, None] * summed).astype(jnp.bfloat16)
    own_expert = lax.axis_index("exp")
    own_index = lax.dynamic_index_in_dim(local_index, own_expert, 0, keepdims=False)
    own_filled = lax.dynamic_index_in_dim(filled, own_expert, 0, keepdims=False)
    placing = (
        (jnp.arange(tokens, dtype=jnp.int32)[:, None] == own_index[None, :]) & own_filled[None, :]
    ).astype(jnp.bfloat16)
    spread = jnp.dot(placing, weighted, preferred_element_type=jnp.float32)
    expert_add = lax.psum_scatter(
        spread.astype(jnp.bfloat16), "exp", scatter_dimension=1, tiled=True
    ).astype(jnp.float32)
    return (hidden_wide + expert_add).astype(jnp.bfloat16)


def solution(mesh):
    return jax.shard_map(
        shards,
        mesh=mesh,
        in_specs=(
            P("seq", "exp"),
            P("seq", "exp"),
            P("seq", "exp"),
            P("seq", "exp"),
            P(),
            P(None, "exp"),
            P("seq"),
            P(None, "exp"),
            P(),
            P(None, "exp"),
            P("exp", None, "seq"),
            P("exp", None, "seq"),
            P("exp", "seq", None),
        ),
        out_specs=P("seq", "exp"),
        check_vma=False,
    )
```

profile of v0, /device:TPU:0, one launch (start us, length us, event | category | flops | bytes accessed | tf_op | source)
XLA Modules:
  0.0 667.6 jit_solution(14505423510101249050)
XLA Ops:
  6.5 0.7 all-gather.5.cloned.1.call-update
  7.3 0.7 all-gather.7.cloned.1.call-update
  8.1 1.5 copy.56
  9.6 0.7 copy.58
  10.2 0.8 dynamic_slice.55
  11.0 125.7 %all-gather.5.cloned.1.call-done = bf16[4096,1024]{1,0:T(8,128)(2,1)} async-done(((bf16[512,1024]{1,0:T(8,128)(2,1)}), bf16[4096,1024]{1,0:T(8,128)(2,1)}) %all-gather.5.cloned.1.call-update) | async-done | bytes 8388624 | tf_op jit(solution)/shard_map/all_gather | solution.py:83
  136.7 11.6 %copy.57 = bf16[8,512,1024]{1,2,0:T(8,128)(2,1)} copy(bf16[8,512,1024]{2,1,0:T(8,128)(2,1)} %bitcast.77) | data formatting | bytes 16777216 | tf_op jit(solution)/shard_map/while | solution.py:94
  148.3 113.2 %all-gather.7.cloned.1.call-done = bf16[4096,1024]{1,0:T(8,128)(2,1)} async-done(((bf16[512,1024]{1,0:T(8,128)(2,1)}), bf16[4096,1024]{1,0:T(8,128)(2,1)}) %all-gather.7.cloned.1.call-update) | async-done | bytes 8388624 | tf_op jit(solution)/shard_map/all_gather | solution.py:84
  261.5 11.4 %copy.59 = bf16[8,512,1024]{1,2,0:T(8,128)(2,1)} copy(bf16[8,512,1024]{2,1,0:T(8,128)(2,1)} %bitcast.78) | data formatting | bytes 16777216 | tf_op jit(solution)/shard_map/while | solution.py:94
  273.1 55.4 %while.18 = (s32[]{:T(128)}, f32[512,8]{0,1:T(8,128)S(1)}, f32[512,8]{0,1:T(8,128)S(1)}, f32[512,8,128]{2,0,1:T(8,128)S(1)}, s32[8]{0:T(128)S(1)}, /*index=5*/s3...) while((s32[]{:T(128)}, f32[512,8]{0,1:T(8,128)S(1)}, ...), condition=%wide.region_5.6_spmd, body=%wide.region_0.5_spmd.sunk | while | flops 1098654208 | bytes 38025672 | solution.py:94
  273.1 0.6 dynamic_slice.64
  274.4 1.3 dynamic_slice.65
  278.7 9.6 %conditional.2 = (f32[512,8]{0,1:T(8,128)S(1)}, f32[512,8]{0,1:T(8,128)S(1)}, f32[512,8,128]{2,0,1:T(8,128)S(1)}) conditional(s32[]{:T(128)} %convert_element_type.103, (s32[]{:T(128)}, s32[512]{0:T(512)S(1)}, s32[4096]{0:T(1024)}, s32[512]{0:T(512)S(1)}, bf16[8,512,1024]{1,2,0:T(8,128)(2,1)}, /*index=5*/s32[]{:T(128)}, ...), branch_computations={%region_1.3_spmd, %region_4.4_spmd} | conditional | flops 1098654208 | bytes 37992520 | solution.py:70
  278.8 0.8 dynamic_slice.47
  279.8 1.7 constant_dynamic-slice_fusion
  281.5 1.7 fusion.2
  283.2 1.7 fusion.1
  285.0 3.4 bitcast_add_fusion
  288.4 0.6 dynamic_slice.64
  289.6 1.3 dynamic_slice.65
  294.1 0.6 dynamic_slice.64
  295.4 1.3 dynamic_slice.65
  299.8 0.6 dynamic_slice.64
  301.1 1.3 dynamic_slice.65
  305.6 0.6 dynamic_slice.64
  306.8 1.3 dynamic_slice.65
  311.3 0.6 dynamic_slice.64
  312.6 1.3 dynamic_slice.65
  317.0 0.6 dynamic_slice.64
  318.3 1.3 dynamic_slice.65
  322.8 0.6 dynamic_slice.64
  324.0 1.3 dynamic_slice.65
  328.5 1.8 copy.60
  330.3 2.8 divide_convert_fusion
  334.3 79.5 %all-gather.9.cloned.1.call-done = bf16[512,4096]{0,1:T(8,128)(2,1)} async-done(((bf16[512,1024]{0,1:T(8,128)(2,1)}), bf16[512,4096]{0,1:T(8,128)(2,1)}) %all-gather.9.cloned.1.call-update) | async-done | bytes 4194320 | tf_op jit(solution)/shard_map/all_gather | solution.py:104
  413.8 14.2 %fusion.18 = (f32[512]{0:T(512)S(1)}, bf16[512,2048]{1,0:T(8,128)(2,1)S(1)}) fusion(bf16[512,4096]{0,1:T(8,128)(2,1)} %all-gather.9.cloned.1.call-done, bf16[4096,2048]{1,0:T(8,128)(2,1)} %param.22, bf16[512,2048]{1,0:T(8,128)(2,1)} %param.17), kind=kOutput, calls=%fused_computation.30 | convolution fusion | flops 8596226048 | bytes 25167872 | tf_op jit(solution)/shard_map/dot_general | solution.py:103
  428.0 5.9 psum.7
  433.9 2.1 fusion.20
  436.0 2.8 gather_fusion
  439.3 8.7 %all_to_all.5 = bf16[16,4,2048]{2,0,1:T(8,128)(2,1)S(1)} all-to-all(bf16[16,4,2048]{2,0,1:T(8,128)(2,1)S(1)} %fusion.34), channel_id=1, replica_groups=mesh['seq'=8,'exp'=4] {'exp'}, dimensions={1} | all-to-all | bytes 524288 | tf_op jit(solution)/shard_map/all_to_all | solution.py:124
  448.0 0.7 copy.67
  448.8 49.2 %all-gather.11.cloned.1.call-done = bf16[128,8192]{1,0:T(8,128)(2,1)} async-done(((bf16[16,8192]{1,0:T(8,128)(2,1)}), bf16[128,8192]{1,0:T(8,128)(2,1)}) %all-gather.11.cloned.1.call-update) | async-done | bytes 2097168 | tf_op jit(solution)/shard_map/all_gather | solution.py:127
  498.0 5.4 fusion.16
  503.5 9.6 %convolution_convert_fusion.1 = bf16[128,8192]{1,0:T(8,128)(2,1)} fusion(bf16[1,512,8192]{2,1,0:T(8,128)(2,1)} %param.29, bf16[128,8192]{1,0:T(8,128)(2,1)S(1)} %copy-done.1, bf16[1,8192,512]{2,1,0:T(8,128)(2,1)} %param.28, f32[128,512]{1,0:T(8,128)S(1)} %fusion.16), kind=kOutput, calls=%fused_computation.21 | convolution fusion | flops 2148925440 | bytes 21233664 | tf_op jit(solution)/shard_map/dot_general | solution.py:132
  513.6 66.4 %reduce-scatter.3.cloned.1.call-done = bf16[16,8192]{1,0:T(8,128)(2,1)} async-done(((bf16[128,8192]{1,0:T(8,128)(2,1)}), bf16[16,8192]{1,0:T(8,128)(2,1)}) %reduce-scatter.3.cloned.1.call-update) | async-done | bytes 262160 | tf_op jit(solution)/shard_map/reduce_scatter | solution.py:131
  580.1 6.6 convolution_convert_fusion
  586.7 70.4 %reduce-scatter.5.cloned.1.call-done = bf16[512,2048]{1,0:T(8,128)(2,1)} async-done(((bf16[512,8192]{1,0:T(8,128)(2,1)}), bf16[512,2048]{1,0:T(8,128)(2,1)}) %reduce-scatter.5.cloned.1.call-update) | async-done | bytes 2097168 | tf_op jit(solution)/shard_map/reduce_scatter | solution.py:145
  657.1 3.7 fusion.21
  (91 shorter events, 12.3 us)
Async XLA Ops:
  6.5 506.9 %copy-start = (bf16[8192,1]{0,1:T(2,128)(2,1)S(1)}, bf16[8192,1]{0,1:T(2,128)(2,1)}, u32[]{:S(2)}) copy-start(bf16[8192,1]{0,1:T(2,128)(2,1)} %param.26) | copy-start | bytes 49156
  6.5 130.1 %all-gather.5.cloned.1.call-start = ((), (), s32[]{:S(2)}) async-start(), calls=%async_computation.3 | async-start | bytes 9437184 | tf_op jit(solution)/shard_map/all_gather | solution.py:83
  7.3 254.2 %all-gather.7.cloned.1.call-start = ((), (), s32[]{:S(2)}) async-start(), calls=%async_computation.4 | async-start | bytes 9437184 | tf_op jit(solution)/shard_map/all_gather | solution.py:84
  8.0 405.8 %all-gather.9.cloned.1.call-start = ((), (), s32[]{:S(2)}) async-start(), calls=%async_computation.5 | async-start | bytes 5242880 | tf_op jit(solution)/shard_map/all_gather | solution.py:104
  328.5 4.9 copy-start.6
  328.5 5.7 copy-start.7
  328.5 5.7 copy-start.5
  333.2 164.8 %all-gather.11.cloned.1.call-start = ((), (), s32[]{:S(2)}) async-start(), calls=%async_computation.6 | async-start | bytes 2359296 | tf_op jit(solution)/shard_map/all_gather | solution.py:127
  428.0 20.8 %copy-start.2 = (bf16[512,2048]{1,0:T(8,128)(2,1)}, bf16[512,2048]{1,0:T(8,128)(2,1)S(1)}, u32[]{:S(2)}) copy-start(bf16[512,2048]{1,0:T(8,128)(2,1)S(1)} %get-tuple-element.425) | copy-start | bytes 6291460
  448.8 131.3 %reduce-scatter.3.cloned.1.call-start = ((), (), s32[]{:S(2)}) async-start(), calls=%async_computation.7 | async-start | bytes 2359296 | tf_op jit(solution)/shard_map/reduce_scatter | solution.py:131
  498.0 5.4 copy-start.1
  503.5 10.0 %copy-start.4 = (bf16[4,2,8,2048]{3,2,0,1:T(8,128)(2,1)S(1)}, bf16[4,2,8,2048]{3,2,0,1:T(8,128)(2,1)}, u32[]{:S(2)}) copy-start(bf16[4,2,8,2048]{3,2,0,1:T(8,128)(2,1)} %copy.67) | copy-start | bytes 786436
  513.1 144.0 %reduce-scatter.5.cloned.1.call-start = ((), (), s32[]{:S(2)}) async-start(), calls=%async_computation.8 | async-start | bytes 10485760 | tf_op jit(solution)/shard_map/reduce_scatter | solution.py:145
  586.6 70.5 %copy-start.3 = (bf16[512,2048]{1,0:T(8,128)(2,1)S(1)}, bf16[512,2048]{1,0:T(8,128)(2,1)}, u32[]{:S(2)}) copy-start(bf16[512,2048]{1,0:T(8,128)(2,1)} %copy-done.2) | copy-start | bytes 6291460
Sparse Core Ops, SparseCore 0:
  9.5 127.1 all-gather.4
  138.8 122.6 all-gather.6
  333.3 80.4 all-gather.8
  448.9 49.0 all-gather.10
  513.2 66.7 reduce-scatter.2
  586.8 70.2 reduce-scatter.4
where the time goes:
time: 669 us; the launch traced here: 668 us
  waiting for transfers between devices  506 us (76%)
  local copies, waits for them, and re-layouts  59.3 us (9%)
  matrix products  41 us (6%)
  loops' own time  20.9 us (3%)
  blocking collectives  14.6 us (2%)
  between operations  13.7 us (2%)
  other arithmetic  11.6 us (2%)
    all_gather x1, waiting for transfers between devices, shards(): key_piece = lax.all_gather(keys, 'seq', axis=0, tiled=True)  126 us
    all_gather x1, waiting for transfers between devices, shards(): value_piece = lax.all_gather(values, 'seq', axis=0, tiled=True)  113 us
    all_gather x1, waiting for transfers between devices, shards(): lax.all_gather(attended, 'exp', axis=1, tiled=True)  79.5 us
    reduce_scatter x1, waiting for transfers between devices, shards(): lax.psum_scatter(spread.astype(jnp.bfloat16), 'exp', scatter_dimension=1,...  70.4 us
    reduce_scatter x1, waiting for transfers between devices, shards(): lax.psum_scatter(jnp.dot(inner_act, w_down[0], preferred_element_type=jnp...  66.4 us
    all_gather x1, waiting for transfers between devices, shards(): piece = lax.all_gather(expert_rows, 'seq', axis=0, tiled=True)  49.2 us
    while x4, local copies, waits for them, and re-layouts, shards(): lax.scan(scan_step, state, (jnp.arange(blocks, dtype=jnp.int32), key_stac...  25.5 us
    another operation x1, loops' own time, shards(): lax.scan(scan_step, state, (jnp.arange(blocks, dtype=jnp.int32), key_stac...  20.7 us
  transfers between devices with their start and end apart: 6, of which 6 were waited for; matrix products, arithmetic and copies ran while one was open for 2% of the time, Pallas kernels for 0%

commit v1 on v0

--- a/solution.py
+++ b/solution.py
@@ -80,7 +80,12 @@
         jnp.zeros((tokens, heads_here, HD), jnp.float32),
     )
     state = initial
-    key_piece = lax.all_gather(keys, "seq", axis=0, tiled=True)
+    ring = [keys]
+    for hop in range(7):
+        ring.append(lax.ppermute(ring[-1], "seq", [(dev, (dev + 1) % 8) for dev in range(8)]))
+    key_piece = jnp.roll(
+        jnp.concatenate(ring[::-1], axis=0), (lax.axis_index("seq") + 1) * ring[0].shape[0], axis=0
+    )
     value_piece = lax.all_gather(values, "seq", axis=0, tiled=True)
     row_count = key_piece.shape[0]
     blocks = row_count // block_rows

time: 669 us -> 734 us (1.097)
  local copies, waits for them, and re-layouts: 59.3 us -> 96.5 us
  waiting for transfers between devices: 506 us -> 531 us
    ppermute x0 -> x7, waiting for transfers between devices: none -> 267 us  [shards(): lax.ppermute(ring[-1], 'seq', [(dev, (dev + 1) % 8) for dev in range(8)])]
    all_gather x1 -> x0, waiting for transfers between devices: 126 us -> none  [shards(): key_piece = lax.all_gather(keys, 'seq', axis=0, tiled=True)]
    all_gather x1, waiting for transfers between devices: 113 us -> 0.01 us  [shards(): value_piece = lax.all_gather(values, 'seq', axis=0, tiled=True)]
    unnamed x17 -> x50, local copies, waits for them, and re-layouts: 1.54 us -> 29.9 us
    dynamic_slice x0 -> x1, local copies, waits for them, and re-layouts: none -> 7.59 us  [shards(): jnp.roll(jnp.concatenate(ring[::-1], axis=0), (lax.axis_index('seq') + 1)...]
  transfers between devices with their start and end apart: 6 -> 12, of which waited for: 6 -> 11; matrix products, arithmetic and copies ran while one was open for 2% -> 7% of each run, Pallas kernels for 0% -> 0%
where the time goes in v1:
time: 734 us; the launch traced here: 732 us
  waiting for transfers between devices  531 us (72%)
  local copies, waits for them, and re-layouts  96.5 us (13%)
  matrix products  41 us (6%)
  loops' own time  20.6 us (3%)
  blocking collectives  14.6 us (2%)
  between operations  13.4 us (2%)
  other arithmetic  11.6 us (2%)
    ppermute x7, waiting for transfers between devices, shards(): lax.ppermute(ring[-1], 'seq', [(dev, (dev + 1) % 8) for dev in range(8)])  267 us
    all_gather x1, waiting for transfers between devices, shards(): lax.all_gather(attended, 'exp', axis=1, tiled=True)  77.2 us
    reduce_scatter x1, waiting for transfers between devices, shards(): lax.psum_scatter(spread.astype(jnp.bfloat16), 'exp', scatter_dimension=1,...  70.5 us
    reduce_scatter x1, waiting for transfers between devices, shards(): lax.psum_scatter(jnp.dot(inner_act, w_down[0], preferred_element_type=jnp...  66.5 us
    all_gather x1, waiting for transfers between devices, shards(): piece = lax.all_gather(expert_rows, 'seq', axis=0, tiled=True)  49.2 us
    unnamed x50, local copies, waits for them, and re-layouts  29.9 us
    while x4, local copies, waits for them, and re-layouts, shards(): lax.scan(scan_step, state, (jnp.arange(blocks, dtype=jnp.int32), key_stac...  26.3 us
    another operation x1, loops' own time, shards(): lax.scan(scan_step, state, (jnp.arange(blocks, dtype=jnp.int32), key_stac...  20.4 us
  transfers between devices with their start and end apart: 12, of which 11 were waited for; matrix products, arithmetic and copies ran while one was open for 7% of the time, Pallas kernels for 0%

profile of v1, /device:TPU:0, one launch (start us, length us, event | category | flops | bytes accessed | tf_op | source)
XLA Modules:
  0.0 732.3 jit_solution(835996140098449053)
XLA Ops:
  7.3 3.0 collective-permute-start
  10.3 37.5 %collective-permute-done = bf16[512,1024]{1,0:T(8,128)(2,1)S(1)} collective-permute-done((bf16[512,1024]{1,0:T(8,128)(2,1)}, bf16[512,1024]{1,0:T(8,128)(2,1)S(1)}, u32[]{:S(2)}, u32[]{:S(2)}) %collective-permute-start) | collective-permute-done | bytes 1048608 | tf_op jit(solution)/shard_map/ppermute | solution.py:85
  47.8 45.2 %collective-permute-done.1 = bf16[512,1024]{1,0:T(8,128)(2,1)S(1)} collective-permute-done((bf16[512,1024]{1,0:T(8,128)(2,1)S(1)}, bf16[512,1024]{1,0:T(8,128)(2,1)S(1)}, u32[]{:S(2)}, u32[]{:S(2)}) %collective-permute-start.1) | collective-permute-done | bytes 1048608 | tf_op jit(solution)/shard_map/ppermute | solution.py:85
  94.0 50.5 %collective-permute-done.2 = bf16[512,1024]{1,0:T(8,128)(2,1)S(1)} collective-permute-done((bf16[512,1024]{1,0:T(8,128)(2,1)S(1)}, bf16[512,1024]{1,0:T(8,128)(2,1)S(1)}, u32[]{:S(2)}, u32[]{:S(2)}) %collective-permute-start.2) | collective-permute-done | bytes 1048608 | tf_op jit(solution)/shard_map/ppermute | solution.py:85
  145.5 50.3 %collective-permute-done.3 = bf16[512,1024]{1,0:T(8,128)(2,1)S(1)} collective-permute-done((bf16[512,1024]{1,0:T(8,128)(2,1)S(1)}, bf16[512,1024]{1,0:T(8,128)(2,1)S(1)}, u32[]{:S(2)}, u32[]{:S(2)}) %collective-permute-start.3) | collective-permute-done | bytes 1048608 | tf_op jit(solution)/shard_map/ppermute | solution.py:85
  196.9 35.2 %collective-permute-done.4 = bf16[512,1024]{1,0:T(8,128)(2,1)S(1)} collective-permute-done((bf16[512,1024]{1,0:T(8,128)(2,1)S(1)}, bf16[512,1024]{1,0:T(8,128)(2,1)S(1)}, u32[]{:S(2)}, u32[]{:S(2)}) %collective-permute-start.4) | collective-permute-done | bytes 1048608 | tf_op jit(solution)/shard_map/ppermute | solution.py:85
  233.1 26.8 %collective-permute-done.5 = bf16[512,1024]{1,0:T(8,128)(2,1)} collective-permute-done((bf16[512,1024]{1,0:T(8,128)(2,1)S(1)}, bf16[512,1024]{1,0:T(8,128)(2,1)}, u32[]{:S(2)}, u32[]{:S(2)}) %collective-permute-start.5) | collective-permute-done | bytes 1048608 | tf_op jit(solution)/shard_map/ppermute | solution.py:85
  259.9 2.3 copy.56
  262.2 1.7 copy.58
  264.9 21.3 %collective-permute-done.6 = bf16[512,1024]{1,0:T(8,128)(2,1)} collective-permute-done((bf16[512,1024]{1,0:T(8,128)(2,1)}, bf16[512,1024]{1,0:T(8,128)(2,1)}, u32[]{:S(2)}, u32[]{:S(2)}) %collective-permute-start.6) | collective-permute-done | bytes 1048608 | tf_op jit(solution)/shard_map/ppermute | solution.py:85
  286.1 2.3 constant_dynamic-update-slice_fusion.15
  288.4 2.3 constant_dynamic-update-slice_fusion.14
  290.7 2.4 constant_dynamic-update-slice_fusion.13
  293.0 2.3 constant_dynamic-update-slice_fusion.12
  299.7 2.3 constant_dynamic-update-slice_fusion.7
  302.0 2.3 constant_dynamic-update-slice_fusion.6
  310.7 7.6 %constant_dynamic-slice_fusion.3 = bf16[4096,1024]{1,0:T(8,128)(2,1)} fusion(bf16[8192,1024]{1,0:T(8,128)(2,1)} %constant_dynamic-update-slice_fusion, s32[]{:T(128)S(6)} %select_n.66), kind=kLoop, calls=%fused_computation.88 | loop fusion | bytes 16777220 | tf_op jit(solution)/shard_map/jit(_roll_dynamic)/dynamic_slice | solution.py:86
  318.3 11.4 %copy.57 = bf16[8,512,1024]{1,2,0:T(8,128)(2,1)} copy(bf16[8,512,1024]{2,1,0:T(8,128)(2,1)} %bitcast.76) | data formatting | bytes 16777216 | tf_op jit(solution)/shard_map/while | solution.py:99
  329.7 11.4 %copy.59 = bf16[8,512,1024]{1,2,0:T(8,128)(2,1)} copy(bf16[8,512,1024]{2,1,0:T(8,128)(2,1)} %bitcast.78) | data formatting | bytes 16777216 | tf_op jit(solution)/shard_map/while | solution.py:99
  341.3 54.4 %while.18 = (s32[]{:T(128)}, f32[512,8]{0,1:T(8,128)S(1)}, f32[512,8]{0,1:T(8,128)S(1)}, f32[512,8,128]{2,0,1:T(8,128)S(1)}, s32[8]{0:T(128)S(1)}, /*index=5*/s3...) while((s32[]{:T(128)}, f32[512,8]{0,1:T(8,128)S(1)}, ...), condition=%wide.region_5.6_spmd, body=%wide.region_0.5_spmd.sunk | while | flops 1098654208 | bytes 38025672 | solution.py:99
  342.5 1.3 dynamic_slice.73
  346.8 9.6 %conditional.2 = (f32[512,8]{0,1:T(8,128)S(1)}, f32[512,8]{0,1:T(8,128)S(1)}, f32[512,8,128]{2,0,1:T(8,128)S(1)}) conditional(s32[]{:T(128)} %convert_element_type.103, (s32[]{:T(128)}, s32[512]{0:T(512)S(1)}, s32[4096]{0:T(1024)}, s32[512]{0:T(512)S(1)}, bf16[8,512,1024]{1,2,0:T(8,128)(2,1)}, /*index=5*/s32[]{:T(128)}, ...), branch_computations={%region_1.3_spmd, %region_4.4_spmd} | conditional | flops 1098654208 | bytes 37992520 | solution.py:70
  347.9 1.7 constant_dynamic-slice_fusion
  349.6 1.7 fusion.2
  351.3 1.7 fusion.1
  353.0 3.4 bitcast_add_fusion
  357.7 1.3 dynamic_slice.73
  363.3 1.3 dynamic_slice.73
  368.9 1.3 dynamic_slice.73
  374.5 1.3 dynamic_slice.73
  380.1 1.3 dynamic_slice.73
  385.7 1.3 dynamic_slice.73
  391.3 1.3 dynamic_slice.73
  395.7 1.8 copy.60
  397.5 2.9 divide_convert_fusion
  401.5 77.2 %all-gather.6.cloned.1.call-done = bf16[512,4096]{0,1:T(8,128)(2,1)} async-done(((bf16[512,1024]{0,1:T(8,128)(2,1)}), bf16[512,4096]{0,1:T(8,128)(2,1)}) %all-gather.6.cloned.1.call-update) | async-done | bytes 4194320 | tf_op jit(solution)/shard_map/all_gather | solution.py:109
  478.7 14.2 %fusion.18 = (f32[512]{0:T(512)S(1)}, bf16[512,2048]{1,0:T(8,128)(2,1)S(1)}) fusion(bf16[512,4096]{0,1:T(8,128)(2,1)} %all-gather.6.cloned.1.call-done, bf16[4096,2048]{1,0:T(8,128)(2,1)} %param.22, bf16[512,2048]{1,0:T(8,128)(2,1)} %param.17), kind=kOutput, calls=%fused_computation.30 | convolution fusion | flops 8596226048 | bytes 25167872 | tf_op jit(solution)/shard_map/dot_general | solution.py:108
  492.8 5.9 psum.7
  498.7 2.1 fusion.20
  500.9 2.8 gather_fusion
  504.2 8.7 %all_to_all.5 = bf16[16,4,2048]{2,0,1:T(8,128)(2,1)S(1)} all-to-all(bf16[16,4,2048]{2,0,1:T(8,128)(2,1)S(1)} %fusion.34), channel_id=1, replica_groups=mesh['seq'=8,'exp'=4] {'exp'}, dimensions={1} | all-to-all | bytes 524288 | tf_op jit(solution)/shard_map/all_to_all | solution.py:129
  513.7 49.2 %all-gather.8.cloned.1.call-done = bf16[128,8192]{1,0:T(8,128)(2,1)} async-done(((bf16[16,8192]{1,0:T(8,128)(2,1)}), bf16[128,8192]{1,0:T(8,128)(2,1)}) %all-gather.8.cloned.1.call-update) | async-done | bytes 2097168 | tf_op jit(solution)/shard_map/all_gather | solution.py:132
  562.9 5.4 fusion.16
  568.3 9.6 %convolution_convert_fusion.1 = bf16[128,8192]{1,0:T(8,128)(2,1)} fusion(bf16[1,512,8192]{2,1,0:T(8,128)(2,1)} %param.29, bf16[128,8192]{1,0:T(8,128)(2,1)S(1)} %copy-done.1, bf16[1,8192,512]{2,1,0:T(8,128)(2,1)} %param.28, f32[128,512]{1,0:T(8,128)S(1)} %fusion.16), kind=kOutput, calls=%fused_computation.21 | convolution fusion | flops 2148925440 | bytes 21233664 | tf_op jit(solution)/shard_map/dot_general | solution.py:137
  578.5 66.5 %reduce-scatter.3.cloned.1.call-done = bf16[16,8192]{1,0:T(8,128)(2,1)} async-done(((bf16[128,8192]{1,0:T(8,128)(2,1)}), bf16[16,8192]{1,0:T(8,128)(2,1)}) %reduce-scatter.3.cloned.1.call-update) | async-done | bytes 262160 | tf_op jit(solution)/shard_map/reduce_scatter | solution.py:136
  645.0 6.6 convolution_convert_fusion
  651.6 70.5 %reduce-scatter.5.cloned.1.call-done = bf16[512,2048]{1,0:T(8,128)(2,1)} async-done(((bf16[512,8192]{1,0:T(8,128)(2,1)}), bf16[512,2048]{1,0:T(8,128)(2,1)}) %reduce-scatter.5.cloned.1.call-update) | async-done | bytes 2097168 | tf_op jit(solution)/shard_map/reduce_scatter | solution.py:150
  722.1 3.7 fusion.21
  (137 shorter events, 34.4 us)
Async XLA Ops:
  6.5 571.7 %copy-start = (bf16[8192,1]{0,1:T(2,128)(2,1)S(1)}, bf16[8192,1]{0,1:T(2,128)(2,1)}, u32[]{:S(2)}) copy-start(bf16[8192,1]{0,1:T(2,128)(2,1)} %param.26) | copy-start | bytes 49156
  6.5 323.1 %all-gather.4.cloned.1.call-start = ((), (), s32[]{:S(2)}) async-start(), calls=%async_computation.3 | async-start | bytes 9437184 | tf_op jit(solution)/shard_map/all_gather | solution.py:89
  7.3 471.4 %all-gather.6.cloned.1.call-start = ((), (), s32[]{:S(2)}) async-start(), calls=%async_computation.4 | async-start | bytes 5242880 | tf_op jit(solution)/shard_map/all_gather | solution.py:109
  7.3 40.5 %collective-permute-start = (bf16[512,1024]{1,0:T(8,128)(2,1)}, bf16[512,1024]{1,0:T(8,128)(2,1)S(1)}, u32[]{:S(2)}, u32[]{:S(2)}) collective-permute-start(bf16[512,1024]{1,0:T(8,128)(2,1)} %param.19), channel_id=1, source_target_pairs={{0,4},{4,8},{8,12},{12,16},{16,20},{20,24},{24,28},{28,0},{1,5},{5... | collective-permute-start | bytes 3145736 | tf_op jit(solution)/shard_map/ppermute | solution.py:85
  47.8 45.2 %collective-permute-start.1 = (bf16[512,1024]{1,0:T(8,128)(2,1)S(1)}, bf16[512,1024]{1,0:T(8,128)(2,1)S(1)}, u32[]{:S(2)}, u32[]{:S(2)}) collective-permute-start(bf16[512,1024]{1,0:T(8,128)(2,1)S(1)} %collective-permute-done), channel_id=1, source_target_pairs={{0,4},{4,8},{8,12},{12,16},{16,20},{20,24},{24,28},{28,0},{1,5},{5... | collective-permute-start | bytes 3145736 | tf_op jit(solution)/shard_map/ppermute | solution.py:85
  93.0 1.0 copy-start.5
  94.0 50.5 %collective-permute-start.2 = (bf16[512,1024]{1,0:T(8,128)(2,1)S(1)}, bf16[512,1024]{1,0:T(8,128)(2,1)S(1)}, u32[]{:S(2)}, u32[]{:S(2)}) collective-permute-start(bf16[512,1024]{1,0:T(8,128)(2,1)S(1)} %collective-permute-done.1), channel_id=1, source_target_pairs={{0,4},{4,8},{8,12},{12,16},{16,20},{20,24},{24,28},{28,0},{1,5},{5... | collective-permute-start | bytes 3145736 | tf_op jit(solution)/shard_map/ppermute | solution.py:85
  144.5 1.0 copy-start.7
  145.5 50.3 %collective-permute-start.3 = (bf16[512,1024]{1,0:T(8,128)(2,1)S(1)}, bf16[512,1024]{1,0:T(8,128)(2,1)S(1)}, u32[]{:S(2)}, u32[]{:S(2)}) collective-permute-start(bf16[512,1024]{1,0:T(8,128)(2,1)S(1)} %collective-permute-done.2), channel_id=1, source_target_pairs={{0,4},{4,8},{8,12},{12,16},{16,20},{20,24},{24,28},{28,0},{1,5},{5... | collective-permute-start | bytes 3145736 | tf_op jit(solution)/shard_map/ppermute | solution.py:85
  195.8 1.1 copy-start.9
  196.9 35.2 %collective-permute-start.4 = (bf16[512,1024]{1,0:T(8,128)(2,1)S(1)}, bf16[512,1024]{1,0:T(8,128)(2,1)S(1)}, u32[]{:S(2)}, u32[]{:S(2)}) collective-permute-start(bf16[512,1024]{1,0:T(8,128)(2,1)S(1)} %collective-permute-done.3), channel_id=1, source_target_pairs={{0,4},{4,8},{8,12},{12,16},{16,20},{20,24},{24,28},{28,0},{1,5},{5... | collective-permute-start | bytes 3145736 | tf_op jit(solution)/shard_map/ppermute | solution.py:85
  232.1 1.0 copy-start.11
  233.1 26.8 %collective-permute-start.5 = (bf16[512,1024]{1,0:T(8,128)(2,1)S(1)}, bf16[512,1024]{1,0:T(8,128)(2,1)}, u32[]{:S(2)}, u32[]{:S(2)}) collective-permute-start(bf16[512,1024]{1,0:T(8,128)(2,1)S(1)} %collective-permute-done.4), channel_id=1, source_target_pairs={{0,4},{4,8},{8,12},{12,16},{16,20},{20,24},{24,28},{28,0},{1,5},{5... | collective-permute-start | bytes 3145736 | tf_op jit(solution)/shard_map/ppermute | solution.py:85
  259.9 26.2 %collective-permute-start.6 = (bf16[512,1024]{1,0:T(8,128)(2,1)}, bf16[512,1024]{1,0:T(8,128)(2,1)}, u32[]{:S(2)}, u32[]{:S(2)}) collective-permute-start(bf16[512,1024]{1,0:T(8,128)(2,1)} %collective-permute-done.5), channel_id=1, source_target_pairs={{0,4},{4,8},{8,12},{12,16},{16,20},{20,24},{24,28},{28,0},{1,5},{5... | collective-permute-start | bytes 3145736 | tf_op jit(solution)/shard_map/ppermute | solution.py:85
  262.2 36.3 %copy-start.4 = (bf16[512,1024]{1,0:T(8,128)(2,1)S(1)}, bf16[512,1024]{1,0:T(8,128)(2,1)}, u32[]{:S(2)}) copy-start(bf16[512,1024]{1,0:T(8,128)(2,1)} %param.19) | copy-start | bytes 3145732
  263.9 31.5 %copy-start.8 = (bf16[512,1024]{1,0:T(8,128)(2,1)S(1)}, bf16[512,1024]{1,0:T(8,128)(2,1)}, u32[]{:S(2)}) copy-start(bf16[512,1024]{1,0:T(8,128)(2,1)} %copy-done.7) | copy-start | bytes 3145732
  263.9 32.5 %copy-start.6 = (bf16[512,1024]{1,0:T(8,128)(2,1)S(1)}, bf16[512,1024]{1,0:T(8,128)(2,1)}, u32[]{:S(2)}) copy-start(bf16[512,1024]{1,0:T(8,128)(2,1)} %copy-done.5) | copy-start | bytes 3145732
  290.7 13.6 %copy-start.12 = (bf16[512,1024]{1,0:T(8,128)(2,1)S(1)}, bf16[512,1024]{1,0:T(8,128)(2,1)}, u32[]{:S(2)}) copy-start(bf16[512,1024]{1,0:T(8,128)(2,1)} %copy-done.11) | copy-start | bytes 3145732
  293.0 12.3 %copy-start.10 = (bf16[512,1024]{1,0:T(8,128)(2,1)S(1)}, bf16[512,1024]{1,0:T(8,128)(2,1)}, u32[]{:S(2)}) copy-start(bf16[512,1024]{1,0:T(8,128)(2,1)} %copy-done.9) | copy-start | bytes 3145732
  395.7 5.0 copy-start.15
  395.7 5.7 copy-start.16
  395.7 5.8 copy-start.14
  400.4 162.4 %all-gather.8.cloned.1.call-start = ((), (), s32[]{:S(2)}) async-start(), calls=%async_computation.5 | async-start | bytes 2359296 | tf_op jit(solution)/shard_map/all_gather | solution.py:132
  492.8 20.8 %copy-start.2 = (bf16[512,2048]{1,0:T(8,128)(2,1)}, bf16[512,2048]{1,0:T(8,128)(2,1)S(1)}, u32[]{:S(2)}) copy-start(bf16[512,2048]{1,0:T(8,128)(2,1)S(1)} %get-tuple-element.425) | copy-start | bytes 6291460
  513.6 131.4 %reduce-scatter.3.cloned.1.call-start = ((), (), s32[]{:S(2)}) async-start(), calls=%async_computation.6 | async-start | bytes 2359296 | tf_op jit(solution)/shard_map/reduce_scatter | solution.py:136
  562.9 5.4 copy-start.1
  568.3 10.0 %copy-start.13 = (bf16[4,2,8,2048]{3,2,0,1:T(8,128)(2,1)S(1)}, bf16[4,2,8,2048]{3,2,0,1:T(8,128)(2,1)}, u32[]{:S(2)}) copy-start(bf16[4,2,8,2048]{3,2,0,1:T(8,128)(2,1)} %copy.67) | copy-start | bytes 786436
  577.9 144.1 %reduce-scatter.5.cloned.1.call-start = ((), (), s32[]{:S(2)}) async-start(), calls=%async_computation.7 | async-start | bytes 10485760 | tf_op jit(solution)/shard_map/reduce_scatter | solution.py:150
  578.5 143.6 %copy-start.3 = (bf16[512,2048]{1,0:T(8,128)(2,1)S(1)}, bf16[512,2048]{1,0:T(8,128)(2,1)}, u32[]{:S(2)}) copy-start(bf16[512,2048]{1,0:T(8,128)(2,1)} %copy-done.2) | copy-start | bytes 6291460
Sparse Core Ops, SparseCore 0:
  9.5 190.4 all-gather.3
  400.5 78.0 all-gather.5
  513.7 49.0 all-gather.7
  578.1 66.8 reduce-scatter.2
  651.7 70.3 reduce-scatter.4
